TPU v7x, 256 devices: a whole 4x4x8 slice. The times are simulated.
256 devices in a mesh: dp: 32 (over y, x, core), mp: 8 (over z).
Axes of the slice: x: 4, y: 4, z: 8, core: 2. Of those that a mesh axis runs over, the one named last changes fastest.
Arguments:
- saved_query: bfloat16 [32768, 4096], P('dp', 'mp'), may hold values from -80 to 80
- saved_key: bfloat16 [32768, 1024], P('dp', 'mp'), may hold values from -16 to 16
- saved_value: bfloat16 [32768, 1024], P('dp', 'mp'), may hold values from -6 to 6
- grad_output: bfloat16 [32768, 4096], P('dp', 'mp'), may hold values from -24 to 24
- unit_server: int32 [1024], P('dp'), may hold values from 0 to 31, as said below
- unit_place: int32 [1024], P('dp'), may hold values from 0 to 31, as said below
- doc_length: int32 [128], P('dp'), may hold values from 1 to 256
- query_weight: bfloat16 [4096, 4096], P(None, 'mp'), may hold values from -0.078125 to 0.078125
- key_weight: bfloat16 [4096, 1024], P(None, 'mp'), may hold values from -0.078125 to 0.078125
- value_weight: bfloat16 [4096, 1024], P(None, 'mp'), may hold values from -0.078125 to 0.078125
Outputs:
- grad_input: float32 [32768, 4096], P('dp', 'mp')
Inputs may be any that keep to these rules, and one draw needn't show every extreme that they name: `unit_server`: each server receives exactly 32 units, exactly one from the units of each device along dp; the units of one document block come from 8 different devices. The pairs (unit_server, unit_place) are all different, so each server's places 0 to 31 are each taken once.
All inputs are finite; a program needn't handle non-finite values.
Results may differ from a plain program's by a relative error of at most 0.011.
Values may be sent and summed in bfloat16 or wider, within the bound.
A program may use at most 128 MiB of HBM per device.

v0:
```python
import math

import jax
import jax.numpy as jnp
from jax import lax
from jax.sharding import PartitionSpec as P

HEAD = 128
DOC_UNITS = 8


def in_one_piece(arrays, axis, split_dim, concat_dim, along):
    widths = [a.shape[along] for a in arrays]
    both = jnp.concatenate(arrays, axis=along)
    out = lax.all_to_all(both, axis, split_axis=split_dim, concat_axis=concat_dim, tiled=True)
    return tuple(jnp.split(out, [sum(widths[:k]) for k in range(1, len(widths))], axis=along))


def tile_backward(query_rows, key_rows, value_rows, grad_rows, length, kv_heads):
    query_count = query_rows.shape[0]
    key_count = key_rows.shape[0]
    group_size = query_rows.shape[1] // (kv_heads * HEAD)
    score_scale = 1.0 / math.sqrt(HEAD)
    queries = query_rows.reshape(query_count, kv_heads, group_size, HEAD)
    keys = key_rows.reshape(key_count, kv_heads, HEAD)
    values = value_rows.reshape(key_count, kv_heads, HEAD)
    query_index = jnp.arange(query_count, dtype=jnp.int32)
    key_index = jnp.arange(key_count, dtype=jnp.int32)
    live_rows = (query_index < length).astype(grad_rows.dtype)
    masked = (grad_rows * live_rows[:, None]).reshape(query_count, kv_heads, group_size, HEAD)
    allowed = (key_index[None, :] <= query_index[:, None]) & (key_index[None, :] < length)
    scores = (
        jnp.einsum("ikgd,jkd->kgij", queries, keys, preferred_element_type=jnp.float32)
        * score_scale
    )
    scores = jnp.where(allowed, scores, -1e30)
    row_peak = jnp.max(scores, axis=-1, keepdims=True)
    expanded = jnp.where(allowed, jnp.exp(scores - row_peak), 0.0)
    attention = expanded / jnp.sum(expanded, axis=-1, keepdims=True)
    attention_low = attention.astype(jnp.bfloat16)
    attended = jnp.einsum(
        "kgij,jkd->ikgd", attention_low, values, preferred_element_type=jnp.float32
    )
    row_delta = jnp.sum(masked * attended, axis=-1)
    prob_grad = jnp.einsum("ikgd,jkd->kgij", masked, values, preferred_element_type=jnp.float32)
    score_grad = attention * (prob_grad - jnp.transpose(row_delta, (1, 2, 0))[..., None])
    score_low = score_grad.astype(jnp.bfloat16)
    query_grad = (
        jnp.einsum("kgij,jkd->ikgd", score_low, keys, preferred_element_type=jnp.float32)
        * score_scale
    )
    key_grad = (
        jnp.einsum("kgij,ikgd->jkd", score_low, queries, preferred_element_type=jnp.float32)
        * score_scale
    )
    value_grad = jnp.einsum(
        "kgij,ikgd->jkd", attention_low, masked, preferred_element_type=jnp.float32
    )
    return (
        query_grad.reshape(query_count, -1),
        key_grad.reshape(key_count, -1),
        value_grad.reshape(key_count, -1),
    )


def project(grads, query_weight, key_weight, value_weight):
    numbers = (((1,), (1,)), ((), ()))
    summed = lax.dot_general(grads[0], query_weight, numbers, preferred_element_type=jnp.float32)
    summed = summed + lax.dot_general(
        grads[1], key_weight, numbers, preferred_element_type=jnp.float32
    )
    return summed + lax.dot_general(
        grads[2], value_weight, numbers, preferred_element_type=jnp.float32
    )


def local(
    saved_query,
    saved_key,
    saved_value,
    grad_output,
    unit_server,
    unit_place,
    doc_length,
    query_weight,
    key_weight,
    value_weight,
):
    server_count = lax.axis_size("dp")
    unit_count = unit_server.shape[0]
    unit_rows = saved_query.shape[0] // unit_count
    block_rows = DOC_UNITS * unit_rows
    doc_count = unit_count // DOC_UNITS
    kv_heads = saved_key.shape[1] // HEAD

    def outgoing(tensor):
        pieces = tensor.reshape(unit_count, unit_rows, tensor.shape[1])
        return (
            jnp.zeros((server_count, unit_rows, tensor.shape[1]), tensor.dtype)
            .at[unit_server]
            .set(pieces)
        )

    places = jnp.full((server_count,), -1, jnp.int32).at[unit_server].set(unit_place)
    arrived = (
        *in_one_piece(
            (
                outgoing(saved_query),
                outgoing(saved_key),
                outgoing(saved_value),
                outgoing(grad_output),
            ),
            "dp",
            0,
            0,
            2,
        ),
        lax.all_to_all(places, "dp", split_axis=0, concat_axis=0, tiled=True),
    )
    matches = arrived[4][None, :] == jnp.arange(unit_count, dtype=jnp.int32)[:, None]
    source = jnp.sum(
        jnp.where(matches, jnp.arange(server_count, dtype=jnp.int32)[None, :], 0), axis=1
    )

    def assemble(tensor):
        return tensor[source].reshape(doc_count, block_rows, tensor.shape[2])

    doc_query = assemble(arrived[0])
    doc_key = assemble(arrived[1])
    doc_value = assemble(arrived[2])
    doc_grad = assemble(arrived[3])
    query_parts = []
    key_parts = []
    value_parts = []
    for doc_index in range(doc_count):
        length = doc_length[doc_index]
        query_total, key_total, value_total = tile_backward(
            doc_query[doc_index],
            doc_key[doc_index],
            doc_value[doc_index],
            doc_grad[doc_index],
            length,
            kv_heads,
        )
        query_parts.append(query_total.astype(jnp.bfloat16))
        key_parts.append(key_total.astype(jnp.bfloat16))
        value_parts.append(value_total.astype(jnp.bfloat16))
    query_units = jnp.concatenate(query_parts, axis=0)
    key_units = jnp.concatenate(key_parts, axis=0)
    value_units = jnp.concatenate(value_parts, axis=0)
    partial_value = project(
        (query_units, key_units, value_units), query_weight, key_weight, value_weight
    )
    columns = lax.psum_scatter(
        partial_value.astype(jnp.bfloat16), "mp", scatter_dimension=1, tiled=True
    ).astype(jnp.float32)
    pieces = columns.reshape(unit_count, unit_rows, columns.shape[-1])
    back = lax.all_to_all(
        jnp.zeros((server_count, unit_rows, columns.shape[-1]), columns.dtype)
        .at[source]
        .set(pieces)
        .astype(jnp.bfloat16),
        "dp",
        split_axis=0,
        concat_axis=0,
        tiled=True,
    ).astype(jnp.float32)
    return back[unit_server].reshape(unit_count * unit_rows, back.shape[2])


def solution(mesh):
    placed = (
        P("dp", "mp"),
        P("dp", "mp"),
        P("dp", "mp"),
        P("dp", "mp"),
        P("dp"),
        P("dp"),
        P("dp"),
        P(None, "mp"),
        P(None, "mp"),
        P(None, "mp"),
    )
    return jax.shard_map(
        local, mesh=mesh, in_specs=placed, out_specs=P("dp", "mp"), check_vma=False
    )
```

profile of v0, /device:TPU:1, one launch (start us, length us, event | category | flops | bytes accessed | tf_op | source)
XLA Modules:
  0.0 309.3 jit_solution(13285686986869703847)
XLA Ops:
  8.8 8.6 %all-to-all-start = ((s32[32,1,1]{2,1,0:T(1,128)}), s32[32,1,1]{2,1,0:T(1,128)S(1)}, u32[]{:S(2)}, u32[]{:S(2)}) async-start(s32[32,1,1]{2,1,0:T(1,128)} %copy.173), calls=%async_computation | async-start | bytes 32768 | tf_op jit(solution)/shard_map/all_to_all | solution.py:118
  17.5 3.6 %scatter_fusion = bf16[32,32,512]{2,1,0:T(8,128)(2,1)S(1)} fusion(bf16[32,32,512]{2,1,0:T(8,128)(2,1)S(1)} %broadcast.238.clone.1, s32[32]{0:T(128)S(1)} %compare_select_fusion.1, bf16[32,32,512]{2,1,0:T(8,128)(2,1)} %bitcast.360), kind=kCustom, calls=%fused_computation.6 | custom fusion | bytes 3145856 | tf_op jit(solution)/shard_map/scatter | solution.py:101
  21.2 3.6 %scatter_fusion.3 = bf16[32,32,512]{2,1,0:T(8,128)(2,1)S(1)} fusion(bf16[32,32,512]{2,1,0:T(8,128)(2,1)S(1)} %broadcast.238.clone, s32[32]{0:T(128)S(1)} %compare_select_fusion.1, bf16[32,32,512]{2,1,0:T(8,128)(2,1)} %bitcast.361), kind=kCustom, calls=%fused_computation.9 | custom fusion | bytes 3145856 | tf_op jit(solution)/shard_map/scatter | solution.py:101
  24.8 2.8 scatter_fusion.1
  28.4 2.8 scatter_fusion.2
  31.3 2.6 pad_maximum_fusion
  33.9 7.6 %all-to-all-start.1 = ((bf16[32,32,1280]{2,1,0:T(8,128)(2,1)}), bf16[32,32,1280]{2,1,0:T(8,128)(2,1)}, u32[]{:S(2)}, u32[]{:S(2)}) async-start(bf16[32,32,1280]{2,1,0:T(8,128)(2,1)} %pad_maximum_fusion), calls=%async_computation.1 | async-start | bytes 5242880 | tf_op jit(solution)/shard_map/all_to_all | solution.py:15
  47.1 1.9 fusion.119
  49.1 1.9 fusion.121
  54.0 21.1 %all-to-all-done.1 = bf16[32,32,1280]{2,1,0:T(8,128)(2,1)} async-done(((bf16[32,32,1280]{2,1,0:T(8,128)(2,1)}), bf16[32,32,1280]{2,1,0:T(8,128)(2,1)}, u32[]{:S(2)}, u32[]{:S(2)}) %all-to-all-start.1) | async-done | bytes 2621472 | tf_op jit(solution)/shard_map/all_to_all | solution.py:15
  75.0 2.7 fusion.141
  77.8 1.8 gather_fusion.3
  79.6 2.0 broadcast_multiply_fusion.7
  114.3 1.8 copy.190
  125.9 1.8 copy.197
  138.8 8.1 %fusion.80 = f32[1024,4096]{1,0:T(8,128)} fusion(bf16[4096,128]{1,0:T(8,128)(2,1)S(1)} %copy-done, bf16[256,128]{0,1:T(8,128)(2,1)S(1)} %fusion.55, bf16[256,128]{0,1:T(8,128)(2,1)S(1)} %copy-done.24, bf16[256,128]{0,1:T(8,128)(2,1)S(1)} %copy-done.23, bf16[256,128]{0,1:T(8,128)(2,1)S(1)} %copy-done.22), kind=kOutput, calls=%fused_computation.121 | convolution fusion | flops 1074790400 | bytes 18087936 | tf_op jit(solution)/shard_map/dot_general | solution.py:69
  146.9 8.1 %fusion.56 = f32[1024,4096]{1,0:T(8,128)} fusion(bf16[4096,512]{1,0:T(8,128)(2,1)S(1)} %copy-done.53, bf16[256,512]{0,1:T(8,128)(2,1)S(1)} %bitcast.373, bf16[256,512]{0,1:T(8,128)(2,1)S(1)} %bitcast.372, bf16[256,512]{0,1:T(8,128)(2,1)S(1)} %bitcast.371, bf16[256,512]{0,1:T(8,128)(2,1)S(1)} %bitcast.370), kind=kOutput, calls=%fused_computation.93 | convolution fusion | flops 4299161600 | bytes 22020096 | tf_op jit(solution)/shard_map/dot_general | solution.py:68
  155.0 15.4 %add_convert_fusion = bf16[1024,4096]{1,0:T(8,128)(2,1)} fusion(f32[1024,4096]{1,0:T(8,128)} %fusion.56, f32[1024,4096]{1,0:T(8,128)} %fusion.80, bf16[4096,128]{1,0:T(8,128)(2,1)S(1)} %copy-done.14, bf16[256,128]{0,1:T(8,128)(2,1)S(1)} %fusion.48, bf16[256,128]{0,1:T(8,128)(2,1)S(1)} %fusion.49, bf16[256,128]{0,1:T(8,128)(2,1)S(1)} %fusion.50, ...), kind=kOutput, calls=%fused_computation.11 | convolution fusion | flops 1087373312 | bytes 43253760 | tf_op jit(solution)/shard_map/dot_general | solution.py:72
  170.4 95.4 %reduce-scatter.2.cloned.1.call-done = bf16[1024,512]{1,0:T(8,128)(2,1)} async-done(((bf16[1024,4096]{1,0:T(8,128)(2,1)}), bf16[1024,512]{1,0:T(8,128)(2,1)}) %reduce-scatter.2.cloned.1.call-update) | async-done | bytes 1048592 | tf_op jit(solution)/shard_map/reduce_scatter | solution.py:154
  265.8 2.8 convert.1
  268.9 4.0 %scatter_fusion.4 = f32[32,32,512]{2,1,0:T(8,128)S(1)} fusion(f32[32,32,512]{2,1,0:T(8,128)S(1)} %broadcast_in_dim.48, s32[32]{0:T(128)S(1)} %copy-done.47, f32[32,32,512]{2,1,0:T(8,128)} %convert.1), kind=kCustom, calls=%fused_computation.10 | custom fusion | bytes 6291584 | tf_op jit(solution)/shard_map/scatter | solution.py:161
  274.1 7.5 %all-to-all-start.2 = ((bf16[32,32,512]{2,1,0:T(8,128)(2,1)}), bf16[32,32,512]{2,1,0:T(8,128)(2,1)}, u32[]{:S(2)}, u32[]{:S(2)}) async-start(bf16[32,32,512]{2,1,0:T(8,128)(2,1)} %convert_element_type.331), calls=%async_computation.3 | async-start | bytes 2097152 | tf_op jit(solution)/shard_map/all_to_all | solution.py:158
  281.6 17.2 %all-to-all-done.2 = bf16[32,32,512]{2,1,0:T(8,128)(2,1)} async-done(((bf16[32,32,512]{2,1,0:T(8,128)(2,1)}), bf16[32,32,512]{2,1,0:T(8,128)(2,1)}, u32[]{:S(2)}, u32[]{:S(2)}) %all-to-all-start.2) | async-done | bytes 1048608 | tf_op jit(solution)/shard_map/all_to_all | solution.py:158
  300.4 2.0 gather_fusion.4
  (196 shorter events, 67.8 us)
Async XLA Ops:
  6.5 131.8 %copy-start = (bf16[4096,128]{1,0:T(8,128)(2,1)S(1)}, bf16[4096,128]{1,0:T(8,128)(2,1)}, u32[]{:S(2)}) copy-start(bf16[4096,128]{1,0:T(8,128)(2,1)} %param.18) | copy-start | bytes 3145732
  7.3 21.1 %copy-start.36 = (s32[32]{0:T(128)}, s32[32]{0:T(128)S(1)}, u32[]{:S(2)}) copy-start(s32[32]{0:T(128)S(1)} %compare_select_fusion.1) | copy-start | bytes 388
  8.8 25.1 %all-to-all-start = ((s32[32,1,1]{2,1,0:T(1,128)}), s32[32,1,1]{2,1,0:T(1,128)S(1)}, u32[]{:S(2)}, u32[]{:S(2)}) async-start(s32[32,1,1]{2,1,0:T(1,128)} %copy.173), calls=%async_computation | async-start | bytes 32768 | tf_op jit(solution)/shard_map/all_to_all | solution.py:118
  33.9 7.8 %copy-start.41 = (s32[4]{0:T(128)S(1)}, s32[4]{0:T(128)}, u32[]{:S(2)}) copy-start(s32[4]{0:T(128)} %param.16) | copy-start | bytes 52
  33.9 41.2 %all-to-all-start.1 = ((bf16[32,32,1280]{2,1,0:T(8,128)(2,1)}), bf16[32,32,1280]{2,1,0:T(8,128)(2,1)}, u32[]{:S(2)}, u32[]{:S(2)}) async-start(bf16[32,32,1280]{2,1,0:T(8,128)(2,1)} %pad_maximum_fusion), calls=%async_computation.1 | async-start | bytes 5242880 | tf_op jit(solution)/shard_map/all_to_all | solution.py:15
  41.4 224.4 %reduce-scatter.2.cloned.1.call-start = ((), (), s32[]{:S(2)}) async-start(), calls=%async_computation.4 | async-start | bytes 9437184 | tf_op jit(solution)/shard_map/reduce_scatter | solution.py:154
  54.0 25.6 %copy-start.38 = (bf16[8,32]{1,0:T(8,128)(2,1)S(1)}, bf16[8,32]{1,0:T(8,128)(2,1)}, u32[]{:S(2)}) copy-start(bf16[8,32]{1,0:T(8,128)(2,1)} %get-tuple-element.49) | copy-start | bytes 1540
  54.0 25.6 %copy-start.39 = (bf16[8,32]{1,0:T(8,128)(2,1)S(1)}, bf16[8,32]{1,0:T(8,128)(2,1)}, u32[]{:S(2)}) copy-start(bf16[8,32]{1,0:T(8,128)(2,1)} %get-tuple-element.50) | copy-start | bytes 1540
  54.0 25.7 %copy-start.40 = (bf16[8,32]{1,0:T(8,128)(2,1)S(1)}, bf16[8,32]{1,0:T(8,128)(2,1)}, u32[]{:S(2)}) copy-start(bf16[8,32]{1,0:T(8,128)(2,1)} %get-tuple-element.51) | copy-start | bytes 1540
  81.6 8.6 %copy-start.4 = (bf16[8,32,512]{2,1,0:T(8,128)(2,1)S(1)}, bf16[8,32,512]{2,1,0:T(8,128)(2,1)}, u32[]{:S(2)}) copy-start(bf16[8,32,512]{2,1,0:T(8,128)(2,1)} %get-tuple-element.13) | copy-start | bytes 786436
  93.2 3.6 %copy-start.13 = (bf16[256,1,4,128]{3,2,0,1:T(4,128)(2,1)S(1)}, bf16[256,1,4,128]{3,2,0,1:T(4,128)(2,1)}, u32[]{:S(2)}) copy-start(bf16[256,1,4,128]{3,2,0,1:T(4,128)(2,1)} %squeeze.33) | copy-start | bytes 786436
  94.1 4.8 %copy-start.7 = (bf16[8,32,512]{2,1,0:T(8,128)(2,1)S(1)}, bf16[8,32,512]{2,1,0:T(8,128)(2,1)}, u32[]{:S(2)}) copy-start(bf16[8,32,512]{2,1,0:T(8,128)(2,1)} %get-tuple-element.9) | copy-start | bytes 786436
  94.1 5.6 %copy-start.17 = (pred[256,256]{0,1:T(8,128)(4,1)S(1)}, pred[256,256]{0,1:T(8,128)(4,1)}, u32[]{:S(2)}) copy-start(pred[256,256]{0,1:T(8,128)(4,1)} %fusion.114) | copy-start | bytes 196612
  96.1 4.2 %copy-start.51 = (bf16[256]{0:T(256)(128)(2,1)S(1)}, bf16[256]{0:T(256)(128)(2,1)}, u32[]{:S(2)}) copy-start(bf16[256]{0:T(256)(128)(2,1)} %get-tuple-element.42) | copy-start | bytes 1540
  101.6 3.0 copy-start.6
  138.8 8.1 %copy-start.25 = (bf16[128,4,256]{2,0,1:T(8,128)(2,1)S(1)}, bf16[128,4,256]{2,0,1:T(8,128)(2,1)}, u32[]{:S(2)}) copy-start(bf16[128,4,256]{2,0,1:T(8,128)(2,1)} %fusion.28) | copy-start | bytes 786436
  138.8 8.1 %copy-start.26 = (bf16[128,4,256]{2,0,1:T(8,128)(2,1)S(1)}, bf16[128,4,256]{2,0,1:T(8,128)(2,1)}, u32[]{:S(2)}) copy-start(bf16[128,4,256]{2,0,1:T(8,128)(2,1)} %fusion.29) | copy-start | bytes 786436
  138.8 8.1 %copy-start.27 = (bf16[128,4,256]{2,0,1:T(8,128)(2,1)S(1)}, bf16[128,4,256]{2,0,1:T(8,128)(2,1)}, u32[]{:S(2)}) copy-start(bf16[128,4,256]{2,0,1:T(8,128)(2,1)} %fusion.30) | copy-start | bytes 786436
  138.8 8.1 %copy-start.53 = (bf16[4096,512]{1,0:T(8,128)(2,1)S(1)}, bf16[4096,512]{1,0:T(8,128)(2,1)}, u32[]{:S(2)}) copy-start(bf16[4096,512]{1,0:T(8,128)(2,1)} %param.17) | copy-start | bytes 12582916
  146.9 8.1 %copy-start.14 = (bf16[4096,128]{1,0:T(8,128)(2,1)S(1)}, bf16[4096,128]{1,0:T(8,128)(2,1)}, u32[]{:S(2)}) copy-start(bf16[4096,128]{1,0:T(8,128)(2,1)} %param.19) | copy-start | bytes 3145732
  265.8 3.1 copy-start.47
  272.9 8.7 %copy-start.37 = (s32[32]{0:T(128)S(1)}, s32[32]{0:T(128)}, u32[]{:S(2)}) copy-start(s32[32]{0:T(128)} %copy-done.36) | copy-start | bytes 388
  274.1 24.8 %all-to-all-start.2 = ((bf16[32,32,512]{2,1,0:T(8,128)(2,1)}), bf16[32,32,512]{2,1,0:T(8,128)(2,1)}, u32[]{:S(2)}, u32[]{:S(2)}) async-start(bf16[32,32,512]{2,1,0:T(8,128)(2,1)} %convert_element_type.331), calls=%async_computation.3 | async-start | bytes 2097152 | tf_op jit(solution)/shard_map/all_to_all | solution.py:158
  298.8 3.6 %copy-start.1 = (bf16[4096,128]{1,0:T(8,128)(2,1)S(1)}, bf16[4096,128]{1,0:T(8,128)(2,1)}, u32[]{:S(2)}) copy-start(bf16[4096,128]{1,0:T(8,128)(2,1)} %param.18) | copy-start | bytes 3145732
  (34 other events, 44.0 us)
Sparse Core Ops, SparseCore 0:
  170.6 95.2 reduce-scatter.1
where the time goes:
time: 311 us; the launch traced here: 309 us
  waiting for transfers between devices  134 us (43%)
  local copies, waits for them, and re-layouts  62.5 us (20%)
  matrix products  49.8 us (16%)
  other arithmetic  25.2 us (8%)
  starting transfers between devices  23.9 us (8%)
  between operations  14.3 us (5%)
    reduce_scatter x1, waiting for transfers between devices, local(): lax.psum_scatter(partial_value.astype(jnp.bfloat16), 'mp', scatter_dimens...  95.4 us
    all_to_all x1, waiting for transfers between devices, in_one_piece(): lax.all_to_all(both, axis, split_axis=split_dim, concat_axis=concat_dim,...  21.1 us
    all_to_all x1, waiting for transfers between devices, local(): lax.all_to_all(jnp.zeros((server_count, unit_rows, columns.shape[-1]), co...  17.2 us
    squeeze x12, local copies, waits for them, and re-layouts, local(): doc_grad[doc_index]  16.3 us
    dot_general x1, matrix products, project(): lax.dot_general(grads[2], value_weight, numbers, preferred_element_type=j...  15.4 us
    scatter x4, local copies, waits for them, and re-layouts, outgoing(): return jnp.zeros((server_count, unit_rows, tensor.shape[1]), tensor.dtype...  12.8 us
    all_to_all x1, starting transfers between devices, local(): lax.all_to_all(places, 'dp', split_axis=0, concat_axis=0, tiled=True)  8.59 us
    dot_general x1, matrix products, project(): lax.dot_general(grads[1], key_weight, numbers, preferred_element_type=jnp...  8.1 us
  transfers between devices with their start and end apart: 4, of which 3 were waited for; matrix products, arithmetic and copies ran while one was open for 9% of the time, Pallas kernels for 0%

commit v1 on v0

v1 whole, which is shorter than its diff:
```python
import functools
import math

import jax
import jax.numpy as jnp
from jax import lax
from jax.experimental import pallas as pl
from jax.experimental.pallas import tpu as pltpu
from jax.sharding import PartitionSpec as P

HEAD = 128
DOC_UNITS = 8
MESH = pl.DeviceIdType.MESH
NT = (((1,), (1,)), ((), ()))
NN = (((1,), (0,)), ((), ()))
TN = (((0,), (0,)), ((), ()))
CHUNK_UNITS = 4
GRID_Y, GRID_X, CORES = 4, 4, 2


def dot(a, b, numbers):
    return lax.dot_general(a, b, numbers, preferred_element_type=jnp.float32)


def kernel(
    n_dp,
    n_mp,
    server_ref,
    place_ref,
    length_ref,
    q_hbm,
    k_hbm,
    v_hbm,
    g_hbm,
    wq_hbm,
    wk_hbm,
    wv_hbm,
    out_hbm,
    in_buf,
    stage,
    recv,
    table_out,
    table_in,
    inv_vec,
    inv_smem,
    where_vec,
    where_smem,
    weights,
    grads,
    lhs,
    ring_send,
    ring_recv,
    out_buf,
    in_sem,
    weight_sem,
    small_sem,
    a2a_send,
    a2a_recv,
    table_send,
    table_recv,
    ring_send_sem,
    ring_recv_sem,
    back_send,
    back_recv,
):
    me = lax.axis_index("dp")
    z = lax.axis_index("mp")
    units, unit_rows, q_cols = q_hbm.shape
    kv_cols = k_hbm.shape[2]
    heads = q_cols // HEAD
    docs = units // DOC_UNITS
    g_at, k_at, v_at = q_cols, 2 * q_cols, 2 * q_cols + kv_cols
    core = lax.rem(me, CORES)
    x = lax.rem(me // CORES, GRID_X)
    y = me // (CORES * GRID_X)

    def peer(offset):
        dc = lax.rem(offset, CORES)
        dx = lax.rem(offset // CORES, GRID_X)
        dy = offset // (CORES * GRID_X)
        return (
            lax.rem(y + dy, GRID_Y) * GRID_X + lax.rem(x + dx, GRID_X)
        ) * CORES + lax.rem(core + dc, CORES)

    loads = [
        pltpu.make_async_copy(q_hbm, in_buf.at[:, :, pl.ds(0, q_cols)], in_sem.at[0]),
        pltpu.make_async_copy(g_hbm, in_buf.at[:, :, pl.ds(g_at, q_cols)], in_sem.at[1]),
        pltpu.make_async_copy(k_hbm, in_buf.at[:, :, pl.ds(k_at, kv_cols)], in_sem.at[2]),
        pltpu.make_async_copy(v_hbm, in_buf.at[:, :, pl.ds(v_at, kv_cols)], in_sem.at[3]),
    ]
    for copy in loads:
        copy.start()
    weight_loads = [
        pltpu.make_async_copy(wq_hbm, weights.at[:, pl.ds(0, q_cols)], weight_sem.at[0]),
        pltpu.make_async_copy(wk_hbm, weights.at[:, pl.ds(q_cols, kv_cols)], weight_sem.at[1]),
        pltpu.make_async_copy(
            wv_hbm, weights.at[:, pl.ds(q_cols + kv_cols, kv_cols)], weight_sem.at[2]
        ),
    ]

    barrier = pltpu.get_barrier_semaphore()

    def greet(o, carry):
        pl.semaphore_signal(barrier, inc=1, device_id={"dp": peer(o)}, device_id_type=MESH)
        return carry

    lax.fori_loop(1, n_dp, greet, 0)
    right, left = lax.rem(z + 1, n_mp), lax.rem(z + n_mp - 1, n_mp)
    for near in (left, right):
        pl.semaphore_signal(barrier, inc=1, device_id={"mp": near}, device_id_type=MESH)

    lanes = lax.broadcasted_iota(jnp.int32, (8, 128), 1)
    unit_of = jnp.zeros((8, 128), jnp.int32)
    place_of = jnp.zeros((8, 128), jnp.int32)
    for u in range(units):
        hit = lanes == server_ref[u]
        unit_of = jnp.where(hit, u, unit_of)
        place_of = jnp.where(hit, place_ref[u], place_of)
    inv_vec[...] = unit_of
    table_out[...] = place_of
    table_in[me] = place_of
    to_smem = pltpu.make_async_copy(inv_vec, inv_smem, small_sem.at[0])
    to_smem.start()
    to_smem.wait()
    for copy in loads:
        copy.wait()

    pl.semaphore_wait(barrier, n_dp - 1 + 2)

    def table_copy(o):
        to = peer(o)
        return pltpu.make_async_remote_copy(
            src_ref=table_out,
            dst_ref=table_in.at[me],
            send_sem=table_send.at[to],
            recv_sem=table_recv.at[me],
            device_id={"dp": to},
            device_id_type=MESH,
        )

    def unit_copy(o):
        to = peer(o)
        return pltpu.make_async_remote_copy(
            src_ref=stage.at[to],
            dst_ref=recv.at[me],
            send_sem=a2a_send.at[to],
            recv_sem=a2a_recv.at[me],
            device_id={"dp": to},
            device_id_type=MESH,
        )

    def send_unit(o, carry):
        table_copy(o).start()
        to = peer(o)
        stage[to] = in_buf[inv_smem[0, to]]
        unit_copy(o).start()
        return carry

    lax.fori_loop(1, n_dp, send_unit, 0)
    recv[me] = in_buf[inv_smem[0, me]]
    for copy in weight_loads:
        copy.start()

    def table_arrived(o, carry):
        frm = peer(o)
        pltpu.make_async_remote_copy(
            src_ref=table_out,
            dst_ref=table_in.at[frm],
            send_sem=table_send.at[frm],
            recv_sem=table_recv.at[frm],
            device_id={"dp": frm},
            device_id_type=MESH,
        ).wait()
        return carry

    lax.fori_loop(1, n_dp, table_arrived, 0)
    table = table_in[:, 0, :]
    wide = lax.broadcasted_iota(jnp.int32, (units, 128), 1)
    tall = lax.broadcasted_iota(jnp.int32, (units, 128), 0)
    place_col = jnp.sum(jnp.where(wide == me, table, 0), axis=1, keepdims=True)
    source = jnp.max(jnp.where(place_col == wide, tall, 0), axis=0, keepdims=True)
    where_vec[pl.ds(0, units), :] = jnp.broadcast_to(place_col, (units, 128))
    where_vec[pl.ds(units, 8), :] = jnp.broadcast_to(source, (8, 128))
    to_smem = pltpu.make_async_copy(where_vec, where_smem, small_sem.at[1])
    to_smem.start()
    to_smem.wait()

    def unit_arrived(o, carry):
        frm = peer(o)
        pltpu.make_async_remote_copy(
            src_ref=stage.at[frm],
            dst_ref=recv.at[frm],
            send_sem=a2a_send.at[frm],
            recv_sem=a2a_recv.at[frm],
            device_id={"dp": frm},
            device_id_type=MESH,
        ).wait()
        return carry

    lax.fori_loop(1, n_dp, unit_arrived, 0)

    block = DOC_UNITS * unit_rows
    score_scale = 1.0 / math.sqrt(HEAD)
    exponent_scale = score_scale * math.log2(math.e)

    def one_doc(doc, carry):
        length = length_ref[doc]
        sources = [where_smem[units, doc * DOC_UNITS + i] for i in range(DOC_UNITS)]

        def rows(at):
            return jnp.concatenate(
                [recv[s, :, pl.ds(at, HEAD)] for s in sources], axis=0
            )

        key_at = lax.broadcasted_iota(jnp.int32, (block, block), 0)
        query_at = lax.broadcasted_iota(jnp.int32, (block, block), 1)
        allowed = (key_at <= query_at) & (key_at < length)
        live = lax.broadcasted_iota(jnp.int32, (block, HEAD), 0) < length
        keys, values = rows(k_at), rows(v_at)
        key_grad = jnp.zeros((block, HEAD), jnp.float32)
        value_grad = jnp.zeros((block, HEAD), jnp.float32)

        def store(at, value):
            low = value.astype(jnp.bfloat16)
            for i in range(DOC_UNITS):
                grads[doc * DOC_UNITS + i, :, pl.ds(at, HEAD)] = low[
                    i * unit_rows : (i + 1) * unit_rows
                ]

        for head in range(heads):
            queries = rows(head * HEAD)
            masked = rows(g_at + head * HEAD)
            masked = jnp.where(live, masked, jnp.zeros_like(masked))
            scores = jnp.where(allowed, dot(keys, queries, NT), -1e30)
            peak = jnp.max(scores, axis=0, keepdims=True)
            expanded = jnp.exp2((scores - peak) * exponent_scale)
            probs = expanded * (1.0 / jnp.sum(expanded, axis=0, keepdims=True))
            probs_low = probs.astype(jnp.bfloat16)
            prob_grad = dot(values, masked, NT)
            delta = jnp.sum(probs_low.astype(jnp.float32) * prob_grad, axis=0, keepdims=True)
            score_low = (probs * (prob_grad - delta)).astype(jnp.bfloat16)
            value_grad += dot(probs_low, masked, NN)
            key_grad += dot(score_low, queries, NN)
            store(head * HEAD, dot(score_low, keys, TN) * score_scale)
        store(q_cols, key_grad * score_scale)
        store(q_cols + kv_cols, value_grad)
        return carry

    lax.fori_loop(0, docs, one_doc, 0)
    for copy in weight_loads:
        copy.wait()

    chunks = units // CHUNK_UNITS
    chunk_rows = CHUNK_UNITS * unit_rows
    half = chunk_rows // 2
    out_cols = out_hbm.shape[2]
    far = n_mp // 2

    def part(chunk, distance, first, count):
        column = lax.rem(z + distance, n_mp) * out_cols
        return dot(
            lhs[chunk, pl.ds(first, count), :],
            weights[pl.ds(pl.multiple_of(column, out_cols), out_cols), :],
            NT,
        )

    def ring_copy(chunk, way, step):
        first, count = (0, chunk_rows) if step else (way * half, half)
        return pltpu.make_async_remote_copy(
            src_ref=ring_send.at[chunk, way, step, pl.ds(first, count), :],
            dst_ref=ring_recv.at[chunk, way, step, pl.ds(first, count), :],
            send_sem=ring_send_sem.at[chunk, way, step],
            recv_sem=ring_recv_sem.at[chunk, way, step],
            device_id={"mp": left if way else right},
            device_id_type=MESH,
        )

    def back_copy(chunk, i):
        to = peer(chunk * CHUNK_UNITS + i)
        return pltpu.make_async_remote_copy(
            src_ref=out_buf.at[chunk * CHUNK_UNITS + i],
            dst_ref=out_hbm.at[me],
            send_sem=back_send.at[to],
            recv_sem=back_recv.at[me],
            device_id={"dp": to},
            device_id_type=MESH,
        )

    own_copy = pltpu.make_async_copy(out_buf.at[0], out_hbm.at[me], small_sem.at[2])

    def slot(t, carry):
        @pl.when(t < chunks)
        def _():
            for i in range(CHUNK_UNITS):
                s = peer(t * CHUNK_UNITS + i)
                lhs[t, pl.ds(i * unit_rows, unit_rows), :] = grads[where_smem[s, 0]]

        for step in range(far):
            chunk = t - step

            @pl.when((chunk >= 0) & (chunk < chunks))
            def _(chunk=chunk, step=step):
                for way in range(2):
                    distance = n_mp - far + step if way else far - step
                    if step == 0:
                        first, count = way * half, half
                        ring_send[chunk, way, step, pl.ds(first, count), :] = part(
                            chunk, distance, first, count
                        ).astype(jnp.bfloat16)
                    else:
                        ring_copy(chunk, way, step - 1).wait_recv()
                        for p in range(2):
                            first, count = p * half, half
                            total = part(chunk, distance, first, count)
                            if step > 1 or p == way:
                                total += ring_recv[
                                    chunk, way, step - 1, pl.ds(first, count), :
                                ].astype(jnp.float32)
                            ring_send[chunk, way, step, pl.ds(first, count), :] = total.astype(
                                jnp.bfloat16
                            )
                    ring_copy(chunk, way, step).start()

        chunk = t - far

        @pl.when(chunk >= 0)
        def _():
            for way in range(2):
                ring_copy(chunk, way, far - 1).wait_recv()
            for i in range(CHUNK_UNITS):
                first = i * unit_rows
                total = part(chunk, 0, first, unit_rows)
                for way in range(2):
                    total += ring_recv[
                        chunk, way, far - 1, pl.ds(first, unit_rows), :
                    ].astype(jnp.float32)
                out_buf[chunk * CHUNK_UNITS + i] = total.astype(jnp.bfloat16)
                if i == 0:

                    @pl.when(chunk == 0)
                    def _():
                        own_copy.start()

                    @pl.when(chunk > 0)
                    def _():
                        back_copy(chunk, 0).start()
                else:
                    back_copy(chunk, i).start()

        return carry

    lax.fori_loop(0, chunks + far, slot, 0)
    own_copy.wait()

    def ring_done(chunk, carry):
        for way in range(2):
            for step in range(far):
                ring_copy(chunk, way, step).wait_send()
        return carry

    lax.fori_loop(0, chunks, ring_done, 0)

    def back_arrived(o, carry):
        frm = peer(o)
        pltpu.make_async_remote_copy(
            src_ref=out_buf.at[o],
            dst_ref=out_hbm.at[frm],
            send_sem=back_send.at[frm],
            recv_sem=back_recv.at[frm],
            device_id={"dp": frm},
            device_id_type=MESH,
        ).wait()
        return carry

    lax.fori_loop(1, n_dp, back_arrived, 0)


def local(
    saved_query,
    saved_key,
    saved_value,
    grad_output,
    unit_server,
    unit_place,
    doc_length,
    query_weight,
    key_weight,
    value_weight,
):
    n_dp, n_mp = lax.axis_size("dp"), lax.axis_size("mp")
    units = unit_server.shape[0]
    unit_rows = saved_query.shape[0] // units
    q_cols, kv_cols = saved_query.shape[1], saved_key.shape[1]
    out_all = query_weight.shape[0]
    out_cols = out_all // n_mp
    k_cols = q_cols + 2 * kv_cols
    in_cols = 2 * q_cols + 2 * kv_cols
    chunks = units // CHUNK_UNITS
    chunk_rows = CHUNK_UNITS * unit_rows
    far = n_mp // 2
    low = jnp.bfloat16

    def split(a):
        return a.reshape(units, unit_rows, a.shape[1])

    smem = pl.BlockSpec(memory_space=pltpu.SMEM)
    hbm = pl.BlockSpec(memory_space=pl.ANY)
    dma = pltpu.SemaphoreType.DMA
    back = pl.pallas_call(
        functools.partial(kernel, n_dp, n_mp),
        out_shape=jax.ShapeDtypeStruct((n_dp, unit_rows, out_cols), low),
        in_specs=[smem] * 3 + [hbm] * 7,
        out_specs=hbm,
        scratch_shapes=[
            pltpu.VMEM((units, unit_rows, in_cols), low),
            pltpu.VMEM((n_dp, unit_rows, in_cols), low),
            pltpu.VMEM((n_dp, unit_rows, in_cols), low),
            pltpu.VMEM((8, 128), jnp.int32),
            pltpu.VMEM((n_dp, 8, 128), jnp.int32),
            pltpu.VMEM((8, 128), jnp.int32),
            pltpu.SMEM((8, 128), jnp.int32),
            pltpu.VMEM((units + 8, 128), jnp.int32),
            pltpu.SMEM((units + 8, 128), jnp.int32),
            pltpu.VMEM((out_all, k_cols), low),
            pltpu.VMEM((units, unit_rows, k_cols), low),
            pltpu.VMEM((chunks, chunk_rows, k_cols), low),
            pltpu.VMEM((chunks, 2, far, chunk_rows, out_cols), low),
            pltpu.VMEM((chunks, 2, far, chunk_rows, out_cols), low),
            pltpu.VMEM((units, unit_rows, out_cols), low),
            dma((4,)),
            dma((3,)),
            dma((3,)),
            dma((n_dp,)),
            dma((n_dp,)),
            dma((n_dp,)),
            dma((n_dp,)),
            dma((chunks, 2, far)),
            dma((chunks, 2, far)),
            dma((n_dp,)),
            dma((n_dp,)),
        ],
        compiler_params=pltpu.CompilerParams(
            collective_id=0, has_side_effects=True, vmem_limit_bytes=60 * 1024 * 1024
        ),
        name="attention_backward_exchange",
    )(
        unit_server,
        unit_place,
        doc_length,
        split(saved_query),
        split(saved_key),
        split(saved_value),
        split(grad_output),
        query_weight,
        key_weight,
        value_weight,
    )
    return back[unit_server].astype(jnp.float32).reshape(units * unit_rows, out_cols)


def solution(mesh):
    placed = (
        P("dp", "mp"),
        P("dp", "mp"),
        P("dp", "mp"),
        P("dp", "mp"),
        P("dp"),
        P("dp"),
        P("dp"),
        P(None, "mp"),
        P(None, "mp"),
        P(None, "mp"),
    )
    return jax.shard_map(
        local, mesh=mesh, in_specs=placed, out_specs=P("dp", "mp"), check_vma=False
    )
```

time: 311 us -> 160 us (0.51)
  Pallas kernels: 0 us -> 156 us
  waiting for transfers between devices: 134 us -> 0 us
  local copies, waits for them, and re-layouts: 62.5 us -> 1.84 us
  matrix products: 49.8 us -> 0 us
  starting transfers between devices: 23.9 us -> 0 us
  other arithmetic: 25.2 us -> 2.34 us
  between operations: 14.3 us -> 0.02 us
    pallas_call x0 -> x1, Pallas kernels: none -> 156 us  [local(): pl.pallas_call(functools.partial(kernel, n_dp, n_mp), out_shape=jax.Shape...]
    reduce_scatter x1 -> x0, waiting for transfers between devices: 95.4 us -> none  [local(): lax.psum_scatter(partial_value.astype(jnp.bfloat16), 'mp', scatter_dimens...]
    dot_general x27 -> x0, matrix products: 49.8 us -> none  [the longest x1 15.4 us: project(): lax.dot_general(grads[2], value_weight, numbers, preferred_element_type=j...]
    all_to_all x3 -> x0, waiting for transfers between devices: 38.3 us -> none  [the longest x1 21.1 us: in_one_piece(): lax.all_to_all(both, axis, split_axis=split_dim, concat_axis=concat_dim,...]
    all_to_all x3 -> x0, starting transfers between devices: 23.7 us -> none  [the longest x1 8.59 us: local(): lax.all_to_all(places, 'dp', split_axis=0, concat_axis=0, tiled=True)]
    scatter x6 -> x0, local copies, waits for them, and re-layouts: 17.6 us -> none  [the longest x4 12.8 us: outgoing(): return jnp.zeros((server_count, unit_rows, tensor.shape[1]), tensor.dtype...]
    squeeze x12 -> x0, local copies, waits for them, and re-layouts: 16.3 us -> none  [local(): doc_grad[doc_index]]
    another operation x12 -> x0, local copies, waits for them, and re-layouts: 6.41 us -> none
  transfers between devices with their start and end apart: 4 -> 0, of which waited for: 3 -> 0; matrix products, arithmetic and copies ran while one was open for 9% -> 0% of each run, Pallas kernels for 0% -> 0%
where the time goes in v1:
time: 160 us
  Pallas kernels  156 us (98%)
  other arithmetic  2.34 us (1%)
  local copies, waits for them, and re-layouts  1.84 us (1%)
    pallas_call x1, Pallas kernels, local(): pl.pallas_call(functools.partial(kernel, n_dp, n_mp), out_shape=jax.Shape...  156 us

profile of v1, /device:TPU:1, one launch (start us, length us, event | category | flops | bytes accessed | tf_op | source)
XLA Modules:
  0.0 160.0 jit_solution(13474848579991573873)
XLA Ops:
  0.0 0.7 compare_select_fusion
  0.7 155.8 %attention_backward_exchange.1 = bf16[32,32,512]{2,1,0:T(8,128)(2,1)} custom-call(s32[32]{0:T(128)} %server_ref.1, s32[32]{0:T(128)} %place_ref.1, s32[4]{0:T(128)} %length_ref.1, bf16[32,32,512]{2,1,0:T(8,128)(2,1)} %bitcast.7, bf16[32,32,128]{2,1,0:T(8,128)(2,1)} %bitcast.9, bf16[32,32,128]{2,1,0:T(8,128)(2,1)} %bitcast.10, bf16[32,32,512]{2,1,0:T(8,128)(2,1)} %bitcast.8, ...), custom_call_target="tpu_custom_call" | custom-call | tf_op jit(solution)/shard_map/attention_backward_exchange/pallas_call | solution.py:409
  156.5 1.8 %gather_fusion = bf16[32,32,512]{2,1,0:T(8,128)(2,1)S(1)} fusion(bf16[32,32,512]{2,1,0:T(8,128)(2,1)} %attention_backward_exchange.1, s32[1024]{0:T(1024)S(1)} %pad_clamp_fusion), kind=kCustom, calls=%fused_computation | custom fusion | bytes 2097280 | tf_op jit(solution)/shard_map/gather | solution.py:458
  158.3 1.7 %bitcast_convert_fusion = f32[1024,512]{1,0:T(8,128)} fusion(bf16[32,32,512]{2,1,0:T(8,128)(2,1)S(1)} %gather_fusion), kind=kLoop, calls=%fused_computation.1 | loop fusion | flops 524288 | bytes 3145728 | tf_op jit(solution)/shard_map/convert_element_type | solution.py:458
  (1 shorter events, 0.0 us)

commit v2 on v1

v2 whole, which is shorter than its diff:
```python
import functools
import math

import jax
import jax.numpy as jnp
from jax import lax
from jax.experimental import pallas as pl
from jax.experimental.pallas import tpu as pltpu
from jax.sharding import PartitionSpec as P

HEAD = 128
DOC_UNITS = 8
MESH = pl.DeviceIdType.MESH
NT = (((1,), (1,)), ((), ()))
NN = (((1,), (0,)), ((), ()))
TN = (((0,), (0,)), ((), ()))
CHUNK_UNITS = 4
SETTLE_STEPS = 4
GRID_Y, GRID_X, CORES = 4, 4, 2


def dot(a, b, numbers):
    return lax.dot_general(a, b, numbers, preferred_element_type=jnp.float32)


def kernel(
    n_dp,
    n_mp,
    phases,
    server_ref,
    place_ref,
    length_ref,
    q_hbm,
    k_hbm,
    v_hbm,
    g_hbm,
    wq_hbm,
    wk_hbm,
    wv_hbm,
    out_hbm,
    *scratch,
):
    count = len(phases)
    held, stage, recv = scratch[:count], scratch[count : 2 * count], scratch[2 * count : 3 * count]
    (
        table_out,
        table_in,
        inv_vec,
        inv_smem,
        where_vec,
        where_smem,
        weights,
        kv_total,
        grads,
        lhs,
        ring_send,
        ring_recv,
        out_buf,
        in_sem,
        weight_sem,
        small_sem,
        a2a_send,
        a2a_recv,
        table_send,
        table_recv,
        ring_send_sem,
        ring_recv_sem,
        back_send,
        back_recv,
    ) = scratch[3 * count :]
    me = lax.axis_index("dp")
    z = lax.axis_index("mp")
    units, unit_rows, q_cols = q_hbm.shape
    kv_cols = k_hbm.shape[2]
    docs = units // DOC_UNITS
    core = lax.rem(me, CORES)
    x = lax.rem(me // CORES, GRID_X)
    y = me // (CORES * GRID_X)

    def peer(offset):
        dc = lax.rem(offset, CORES)
        dx = lax.rem(offset // CORES, GRID_X)
        dy = offset // (CORES * GRID_X)
        return (
            lax.rem(y + dy, GRID_Y) * GRID_X + lax.rem(x + dx, GRID_X)
        ) * CORES + lax.rem(core + dc, CORES)

    loads = []
    for p, heads in enumerate(phases):
        pieces = [] if p else [(k_hbm, 0, kv_cols), (v_hbm, 0, kv_cols)]
        for head in heads:
            pieces += [(q_hbm, head * HEAD, HEAD), (g_hbm, head * HEAD, HEAD)]
        at = 0
        for n, (ref, first, width) in enumerate(pieces):
            loads.append(
                (
                    p,
                    pltpu.make_async_copy(
                        ref.at[:, :, pl.ds(first, width)],
                        held[p].at[:, :, pl.ds(at, width)],
                        in_sem.at[len(loads)],
                    ),
                )
            )
            at += width
    for _, copy in loads:
        copy.start()
    weight_loads = [
        pltpu.make_async_copy(wq_hbm, weights.at[:, pl.ds(0, q_cols)], weight_sem.at[0]),
        pltpu.make_async_copy(wk_hbm, weights.at[:, pl.ds(q_cols, kv_cols)], weight_sem.at[1]),
        pltpu.make_async_copy(
            wv_hbm, weights.at[:, pl.ds(q_cols + kv_cols, kv_cols)], weight_sem.at[2]
        ),
    ]

    barrier = pltpu.get_barrier_semaphore()

    def greet(o, carry):
        pl.semaphore_signal(barrier, inc=1, device_id={"dp": peer(o)}, device_id_type=MESH)
        return carry

    lax.fori_loop(1, n_dp, greet, 0)
    right, left = lax.rem(z + 1, n_mp), lax.rem(z + n_mp - 1, n_mp)
    for near in (left, right):
        pl.semaphore_signal(barrier, inc=1, device_id={"mp": near}, device_id_type=MESH)

    lanes = lax.broadcasted_iota(jnp.int32, (8, 128), 1)
    unit_of = jnp.zeros((8, 128), jnp.int32)
    place_of = jnp.zeros((8, 128), jnp.int32)
    for u in range(units):
        hit = lanes == server_ref[u]
        unit_of = jnp.where(hit, u, unit_of)
        place_of = jnp.where(hit, place_ref[u], place_of)
    inv_vec[...] = unit_of
    table_out[...] = place_of
    table_in[me] = place_of
    to_smem = pltpu.make_async_copy(inv_vec, inv_smem, small_sem.at[0])
    to_smem.start()
    to_smem.wait()

    pl.semaphore_wait(barrier, n_dp - 1 + 2)

    def mixed(i):
        return 1 + lax.rem(i * 11 + 5, n_dp - 1)

    def table_copy(o):
        to = peer(o)
        return pltpu.make_async_remote_copy(
            src_ref=table_out,
            dst_ref=table_in.at[me],
            send_sem=table_send.at[to],
            recv_sem=table_recv.at[me],
            device_id={"dp": to},
            device_id_type=MESH,
        )

    for p in range(count):
        for q, copy in loads:
            if p == q:
                copy.wait()

        def send_unit(i, carry, p=p):
            to = peer(mixed(i))
            stage[p][to] = held[p][inv_smem[0, to]]
            pltpu.make_async_remote_copy(
                src_ref=stage[p].at[to],
                dst_ref=recv[p].at[me],
                send_sem=a2a_send.at[p, to],
                recv_sem=a2a_recv.at[p, me],
                device_id={"dp": to},
                device_id_type=MESH,
            ).start()
            if p == 0:
                table_copy(mixed(i)).start()
            return carry

        lax.fori_loop(0, n_dp - 1, send_unit, 0)
        recv[p][me] = held[p][inv_smem[0, me]]
    for copy in weight_loads:
        copy.start()

    def table_arrived(o, carry):
        frm = peer(o)
        pltpu.make_async_remote_copy(
            src_ref=table_out,
            dst_ref=table_in.at[frm],
            send_sem=table_send.at[frm],
            recv_sem=table_recv.at[frm],
            device_id={"dp": frm},
            device_id_type=MESH,
        ).wait()
        return carry

    lax.fori_loop(1, n_dp, table_arrived, 0)
    table = table_in[:, 0, :]
    wide = lax.broadcasted_iota(jnp.int32, (units, 128), 1)
    tall = lax.broadcasted_iota(jnp.int32, (units, 128), 0)
    place_col = jnp.sum(jnp.where(wide == me, table, 0), axis=1, keepdims=True)
    source = jnp.max(jnp.where(place_col == wide, tall, 0), axis=0, keepdims=True)
    where_vec[pl.ds(0, units), :] = jnp.broadcast_to(place_col, (units, 128))
    where_vec[pl.ds(units, 8), :] = jnp.broadcast_to(source, (8, 128))
    to_smem = pltpu.make_async_copy(where_vec, where_smem, small_sem.at[1])
    to_smem.start()
    to_smem.wait()

    block = DOC_UNITS * unit_rows
    score_scale = 1.0 / math.sqrt(HEAD)
    exponent_scale = score_scale * math.log2(math.e)

    def one_doc(p, doc):
        length = length_ref[doc]
        sources = [where_smem[units, doc * DOC_UNITS + i] for i in range(DOC_UNITS)]

        def rows(p, at):
            return jnp.concatenate(
                [recv[p][s, :, pl.ds(at, HEAD)] for s in sources], axis=0
            )

        key_at = lax.broadcasted_iota(jnp.int32, (block, block), 0)
        query_at = lax.broadcasted_iota(jnp.int32, (block, block), 1)
        allowed = (key_at <= query_at) & (key_at < length)
        live = lax.broadcasted_iota(jnp.int32, (block, HEAD), 0) < length
        keys, values = rows(0, 0), rows(0, kv_cols)
        if p == 0:
            key_grad = jnp.zeros((block, HEAD), jnp.float32)
            value_grad = jnp.zeros((block, HEAD), jnp.float32)
        else:
            key_grad, value_grad = kv_total[doc, 0], kv_total[doc, 1]

        def store(at, value):
            low = value.astype(jnp.bfloat16)
            for i in range(DOC_UNITS):
                grads[doc * DOC_UNITS + i, :, pl.ds(at, HEAD)] = low[
                    i * unit_rows : (i + 1) * unit_rows
                ]

        for n, head in enumerate(phases[p]):
            at = 2 * n * HEAD + (0 if p else 2 * kv_cols)
            queries = rows(p, at)
            masked = rows(p, at + HEAD)
            masked = jnp.where(live, masked, jnp.zeros_like(masked))
            scores = jnp.where(allowed, dot(keys, queries, NT), -1e30)
            peak = jnp.max(scores, axis=0, keepdims=True)
            expanded = jnp.exp2((scores - peak) * exponent_scale)
            probs = expanded * (1.0 / jnp.sum(expanded, axis=0, keepdims=True))
            probs_low = probs.astype(jnp.bfloat16)
            prob_grad = dot(values, masked, NT)
            delta = jnp.sum(probs_low.astype(jnp.float32) * prob_grad, axis=0, keepdims=True)
            score_low = (probs * (prob_grad - delta)).astype(jnp.bfloat16)
            value_grad += dot(probs_low, masked, NN)
            key_grad += dot(score_low, queries, NN)
            store(head * HEAD, dot(score_low, keys, TN) * score_scale)
        if p == count - 1:
            store(q_cols, key_grad * score_scale)
            store(q_cols + kv_cols, value_grad)
        else:
            kv_total[doc, 0] = key_grad
            kv_total[doc, 1] = value_grad

    for p in range(count):

        def unit_arrived(o, carry, p=p):
            frm = peer(o)
            pltpu.make_async_remote_copy(
                src_ref=stage[p].at[frm],
                dst_ref=recv[p].at[frm],
                send_sem=a2a_send.at[p, frm],
                recv_sem=a2a_recv.at[p, frm],
                device_id={"dp": frm},
                device_id_type=MESH,
            ).wait()
            return carry

        lax.fori_loop(1, n_dp, unit_arrived, 0)

        def doc_phase(doc, carry, p=p):
            one_doc(p, doc)
            return carry

        lax.fori_loop(0, docs, doc_phase, 0)
    for copy in weight_loads:
        copy.wait()

    chunks = units // CHUNK_UNITS
    chunk_rows = CHUNK_UNITS * unit_rows
    half = chunk_rows // 2
    out_cols = out_hbm.shape[2]
    far = n_mp // 2

    def part(chunk, distance):
        column = lax.rem(z + distance, n_mp) * out_cols
        return dot(
            lhs[chunk],
            weights[pl.ds(pl.multiple_of(column, out_cols), out_cols), :],
            NT,
        )

    def ring_copy(chunk, way, step):
        first, count = (0, chunk_rows) if step else (way * half, half)
        return pltpu.make_async_remote_copy(
            src_ref=ring_send.at[chunk, way, step, pl.ds(first, count), :],
            dst_ref=ring_recv.at[chunk, way, step, pl.ds(first, count), :],
            send_sem=ring_send_sem.at[chunk, way, step],
            recv_sem=ring_recv_sem.at[chunk, way, step],
            device_id={"mp": left if way else right},
            device_id_type=MESH,
        )

    def back_copy(o):
        to = peer(o)
        return pltpu.make_async_remote_copy(
            src_ref=out_buf.at[o],
            dst_ref=out_hbm.at[me],
            send_sem=back_send.at[to],
            recv_sem=back_recv.at[me],
            device_id={"dp": to},
            device_id_type=MESH,
        )

    def first_step(chunk, carry):
        for i in range(CHUNK_UNITS):
            s = peer(chunk * CHUNK_UNITS + i)
            lhs[chunk, pl.ds(i * unit_rows, unit_rows), :] = grads[where_smem[s, 0]]
        low = part(chunk, far).astype(jnp.bfloat16)
        for way in range(2):
            ring_send[chunk, way, 0, pl.ds(way * half, half), :] = low[
                way * half : (way + 1) * half
            ]
            ring_copy(chunk, way, 0).start()
        return carry

    lax.fori_loop(0, chunks, first_step, 0)

    for step in range(1, far):

        def next_step(chunk, carry, step=step):
            for way in range(2):
                total = part(chunk, n_mp - far + step if way else far - step)
                ring_copy(chunk, way, step - 1).wait_recv()
                for h in range(2):
                    piece = total[h * half : (h + 1) * half]
                    if step > 1 or h == way:
                        piece += ring_recv[
                            chunk, way, step - 1, pl.ds(h * half, half), :
                        ].astype(jnp.float32)
                    ring_send[chunk, way, step, pl.ds(h * half, half), :] = piece.astype(
                        jnp.bfloat16
                    )
                ring_copy(chunk, way, step).start()
            return carry

        lax.fori_loop(0, chunks, next_step, 0)

    own_copy = pltpu.make_async_copy(out_buf.at[0], out_hbm.at[me], small_sem.at[2])

    def last_step(chunk, carry):
        total = part(chunk, 0)
        for way in range(2):
            ring_copy(chunk, way, far - 1).wait_recv()
            total += ring_recv[chunk, way, far - 1].astype(jnp.float32)
        low = total.astype(jnp.bfloat16)
        for i in range(CHUNK_UNITS):
            out_buf[chunk * CHUNK_UNITS + i] = low[i * unit_rows : (i + 1) * unit_rows]
        for i in range(CHUNK_UNITS):
            if i == 0:

                @pl.when(chunk == 0)
                def _():
                    own_copy.start()

                @pl.when(chunk > 0)
                def _():
                    back_copy(chunk * CHUNK_UNITS).start()
            else:
                back_copy(chunk * CHUNK_UNITS + i).start()
        return carry

    lax.fori_loop(0, chunks, last_step, 0)
    own_copy.wait()

    def ring_done(chunk, carry):
        for way in range(2):
            for step in range(far):
                ring_copy(chunk, way, step).wait_send()
        return carry

    lax.fori_loop(0, chunks, ring_done, 0)

    def back_arrived(o, carry):
        frm = peer(o)
        pltpu.make_async_remote_copy(
            src_ref=out_buf.at[o],
            dst_ref=out_hbm.at[frm],
            send_sem=back_send.at[frm],
            recv_sem=back_recv.at[frm],
            device_id={"dp": frm},
            device_id_type=MESH,
        ).wait()
        return carry

    lax.fori_loop(1, n_dp, back_arrived, 0)


def settle(server_ref, back_ref, out_ref):
    unit_rows = back_ref.shape[1]
    count = out_ref.shape[0] // unit_rows
    for i in range(count):
        u = pl.program_id(0) * count + i
        out_ref[pl.ds(i * unit_rows, unit_rows), :] = back_ref[server_ref[u]].astype(jnp.float32)


def local(
    saved_query,
    saved_key,
    saved_value,
    grad_output,
    unit_server,
    unit_place,
    doc_length,
    query_weight,
    key_weight,
    value_weight,
):
    n_dp, n_mp = lax.axis_size("dp"), lax.axis_size("mp")
    units = unit_server.shape[0]
    unit_rows = saved_query.shape[0] // units
    q_cols, kv_cols = saved_query.shape[1], saved_key.shape[1]
    out_all = query_weight.shape[0]
    out_cols = out_all // n_mp
    k_cols = q_cols + 2 * kv_cols
    heads = q_cols // HEAD
    phases = [range(0, heads - 2), range(heads - 2, heads - 1), range(heads - 1, heads)]
    widths = [2 * HEAD * len(p) for p in phases]
    widths[0] += 2 * kv_cols
    chunks = units // CHUNK_UNITS
    chunk_rows = CHUNK_UNITS * unit_rows
    far = n_mp // 2
    low = jnp.bfloat16

    def split(a):
        return a.reshape(units, unit_rows, a.shape[1])

    smem = pl.BlockSpec(memory_space=pltpu.SMEM)
    hbm = pl.BlockSpec(memory_space=pl.ANY)
    dma = pltpu.SemaphoreType.DMA
    back = pl.pallas_call(
        functools.partial(kernel, n_dp, n_mp, phases),
        out_shape=jax.ShapeDtypeStruct((n_dp, unit_rows, out_cols), low),
        in_specs=[smem] * 3 + [hbm] * 7,
        out_specs=hbm,
        scratch_shapes=[
            *[pltpu.VMEM((units, unit_rows, w), low) for w in widths],
            *[pltpu.VMEM((n_dp, unit_rows, w), low) for w in widths],
            *[pltpu.VMEM((n_dp, unit_rows, w), low) for w in widths],
            pltpu.VMEM((8, 128), jnp.int32),
            pltpu.VMEM((n_dp, 8, 128), jnp.int32),
            pltpu.VMEM((8, 128), jnp.int32),
            pltpu.SMEM((8, 128), jnp.int32),
            pltpu.VMEM((units + 8, 128), jnp.int32),
            pltpu.SMEM((units + 8, 128), jnp.int32),
            pltpu.VMEM((out_all, k_cols), low),
            pltpu.VMEM((units // DOC_UNITS, 2, DOC_UNITS * unit_rows, HEAD), jnp.float32),
            pltpu.VMEM((units, unit_rows, k_cols), low),
            pltpu.VMEM((chunks, chunk_rows, k_cols), low),
            pltpu.VMEM((chunks, 2, far, chunk_rows, out_cols), low),
            pltpu.VMEM((chunks, 2, far, chunk_rows, out_cols), low),
            pltpu.VMEM((units, unit_rows, out_cols), low),
            dma((2 + 2 * heads,)),
            dma((3,)),
            dma((3,)),
            dma((len(phases), n_dp)),
            dma((len(phases), n_dp)),
            dma((n_dp,)),
            dma((n_dp,)),
            dma((chunks, 2, far)),
            dma((chunks, 2, far)),
            dma((n_dp,)),
            dma((n_dp,)),
        ],
        compiler_params=pltpu.CompilerParams(
            collective_id=0, has_side_effects=True, vmem_limit_bytes=60 * 1024 * 1024
        ),
        name="attention_backward_exchange",
    )(
        unit_server,
        unit_place,
        doc_length,
        split(saved_query),
        split(saved_key),
        split(saved_value),
        split(grad_output),
        query_weight,
        key_weight,
        value_weight,
    )
    rows = units * unit_rows // SETTLE_STEPS
    return pl.pallas_call(
        settle,
        out_shape=jax.ShapeDtypeStruct((units * unit_rows, out_cols), jnp.float32),
        grid_spec=pltpu.PrefetchScalarGridSpec(
            num_scalar_prefetch=1,
            grid=(SETTLE_STEPS,),
            in_specs=[pl.BlockSpec(back.shape, lambda i, server: (0, 0, 0))],
            out_specs=pl.BlockSpec((rows, out_cols), lambda i, server: (i, 0)),
        ),
        name="settle_rows",
    )(unit_server, back)


def solution(mesh):
    placed = (
        P("dp", "mp"),
        P("dp", "mp"),
        P("dp", "mp"),
        P("dp", "mp"),
        P("dp"),
        P("dp"),
        P("dp"),
        P(None, "mp"),
        P(None, "mp"),
        P(None, "mp"),
    )
    return jax.shard_map(
        local, mesh=mesh, in_specs=placed, out_specs=P("dp", "mp"), check_vma=False
    )
```

time: 160 us -> 142 us (0.89)
  Pallas kernels: 156 us -> 142 us
  other arithmetic: 2.34 us -> 0 us
  local copies, waits for them, and re-layouts: 1.84 us -> 0 us
    pallas_call x1 -> x2, Pallas kernels: 156 us -> 142 us  [the longest x1 139 us: local(): pl.pallas_call(functools.partial(kernel, n_dp, n_mp, phases), out_shape=j...]
    gather x1 -> x0, local copies, waits for them, and re-layouts: 1.84 us -> none  [local(): back[unit_server].astype(jnp.float32).reshape(units * unit_rows, out_cols)]
    convert_element_type x1 -> x0, other arithmetic: 1.68 us -> none  [local(): back[unit_server].astype(jnp.float32).reshape(units * unit_rows, out_cols)]
where the time goes in v2:
time: 142 us
  Pallas kernels  142 us (100%)
    pallas_call x1, Pallas kernels, local(): pl.pallas_call(functools.partial(kernel, n_dp, n_mp, phases), out_shape=j...  139 us
    pallas_call x1, Pallas kernels, local(): pl.pallas_call(settle, out_shape=jax.ShapeDtypeStruct((units * unit_rows,...  3.74 us

profile of v2, /device:TPU:1, one launch (start us, length us, event | category | flops | bytes accessed | tf_op | source)
XLA Modules:
  0.0 142.3 jit_solution(16570379695404596876)
XLA Ops:
  0.0 138.6 %attention_backward_exchange.1.back_ref = bf16[32,32,512]{2,1,0:T(8,128)(2,1)} custom-call(s32[32]{0:T(128)} %server_ref.3, s32[32]{0:T(128)} %place_ref.1, s32[4]{0:T(128)} %length_ref.1, bf16[32,32,512]{2,1,0:T(8,128)(2,1)} %bitcast.4, bf16[32,32,128]{2,1,0:T(8,128)(2,1)} %bitcast.6, bf16[32,32,128]{2,1,0:T(8,128)(2,1)} %bitcast.7, ...), custom_call_target="tpu_custom_call" | custom-call | tf_op jit(solution)/shard_map/attention_backward_exchange/pallas_call | solution.py:446
  138.6 3.7 %settle_rows.1 = f32[1024,512]{1,0:T(8,128)} custom-call(s32[32]{0:T(128)} %server_ref.3, bf16[32,32,512]{2,1,0:T(8,128)(2,1)} %attention_backward_exchange.1.back_ref), custom_call_target="tpu_custom_call" | custom-call | tf_op jit(solution)/shard_map/settle_rows/pallas_call | solution.py:497

commit v3 on v2

--- a/solution.py
+++ b/solution.py
@@ -132,8 +132,8 @@
         unit_of = jnp.where(hit, u, unit_of)
         place_of = jnp.where(hit, place_ref[u], place_of)
     inv_vec[...] = unit_of
-    table_out[...] = place_of
-    table_in[me] = place_of
+    table_out[...] = place_of[:1]
+    table_in[me] = place_of[:1]
     to_smem = pltpu.make_async_copy(inv_vec, inv_smem, small_sem.at[0])
     to_smem.start()
     to_smem.wait()
@@ -307,7 +307,7 @@
         )
 
     def back_copy(o):
-        to = peer(o)
+        to = peer(n_dp - 1 - o)
         return pltpu.make_async_remote_copy(
             src_ref=out_buf.at[o],
             dst_ref=out_hbm.at[me],
@@ -319,7 +319,7 @@
 
     def first_step(chunk, carry):
         for i in range(CHUNK_UNITS):
-            s = peer(chunk * CHUNK_UNITS + i)
+            s = peer(n_dp - 1 - (chunk * CHUNK_UNITS + i))
             lhs[chunk, pl.ds(i * unit_rows, unit_rows), :] = grads[where_smem[s, 0]]
         low = part(chunk, far).astype(jnp.bfloat16)
         for way in range(2):
@@ -351,7 +351,7 @@
 
         lax.fori_loop(0, chunks, next_step, 0)
 
-    own_copy = pltpu.make_async_copy(out_buf.at[0], out_hbm.at[me], small_sem.at[2])
+    own_copy = pltpu.make_async_copy(out_buf.at[n_dp - 1], out_hbm.at[me], small_sem.at[2])
 
     def last_step(chunk, carry):
         total = part(chunk, 0)
@@ -361,18 +361,17 @@
         low = total.astype(jnp.bfloat16)
         for i in range(CHUNK_UNITS):
             out_buf[chunk * CHUNK_UNITS + i] = low[i * unit_rows : (i + 1) * unit_rows]
-        for i in range(CHUNK_UNITS):
-            if i == 0:
-
-                @pl.when(chunk == 0)
-                def _():
-                    own_copy.start()
-
-                @pl.when(chunk > 0)
-                def _():
-                    back_copy(chunk * CHUNK_UNITS).start()
-            else:
-                back_copy(chunk * CHUNK_UNITS + i).start()
+        for i in range(CHUNK_UNITS - 1):
+            back_copy(chunk * CHUNK_UNITS + i).start()
+
+        @pl.when(chunk < chunks - 1)
+        def _():
+            back_copy(chunk * CHUNK_UNITS + CHUNK_UNITS - 1).start()
+
+        @pl.when(chunk == chunks - 1)
+        def _():
+            own_copy.start()
+
         return carry
 
     lax.fori_loop(0, chunks, last_step, 0)
@@ -401,12 +400,26 @@
     lax.fori_loop(1, n_dp, back_arrived, 0)
 
 
-def settle(server_ref, back_ref, out_ref):
-    unit_rows = back_ref.shape[1]
-    count = out_ref.shape[0] // unit_rows
-    for i in range(count):
-        u = pl.program_id(0) * count + i
-        out_ref[pl.ds(i * unit_rows, unit_rows), :] = back_ref[server_ref[u]].astype(jnp.float32)
+def settle(server_ref, back_hbm, out_hbm, held, wide, in_sem, out_sem):
+    units, unit_rows = held.shape[:2]
+    rows = units * unit_rows // SETTLE_STEPS
+
+    def fetch(u):
+        return pltpu.make_async_copy(back_hbm.at[server_ref[u]], held.at[u], in_sem.at[u])
+
+    def emit(step):
+        part = pl.ds(step * rows, rows)
+        return pltpu.make_async_copy(wide.at[part, :], out_hbm.at[part, :], out_sem.at[step])
+
+    for u in range(units):
+        fetch(u).start()
+    for step in range(SETTLE_STEPS):
+        for u in range(step * units // SETTLE_STEPS, (step + 1) * units // SETTLE_STEPS):
+            fetch(u).wait()
+            wide[pl.ds(u * unit_rows, unit_rows), :] = held[u].astype(jnp.float32)
+        emit(step).start()
+    for step in range(SETTLE_STEPS):
+        emit(step).wait()
 
 
 def local(
@@ -452,8 +465,8 @@
             *[pltpu.VMEM((units, unit_rows, w), low) for w in widths],
             *[pltpu.VMEM((n_dp, unit_rows, w), low) for w in widths],
             *[pltpu.VMEM((n_dp, unit_rows, w), low) for w in widths],
-            pltpu.VMEM((8, 128), jnp.int32),
-            pltpu.VMEM((n_dp, 8, 128), jnp.int32),
+            pltpu.VMEM((1, 128), jnp.int32),
+            pltpu.VMEM((n_dp, 1, 128), jnp.int32),
             pltpu.VMEM((8, 128), jnp.int32),
             pltpu.SMEM((8, 128), jnp.int32),
             pltpu.VMEM((units + 8, 128), jnp.int32),
@@ -493,16 +506,17 @@
         key_weight,
         value_weight,
     )
-    rows = units * unit_rows // SETTLE_STEPS
     return pl.pallas_call(
         settle,
         out_shape=jax.ShapeDtypeStruct((units * unit_rows, out_cols), jnp.float32),
-        grid_spec=pltpu.PrefetchScalarGridSpec(
-            num_scalar_prefetch=1,
-            grid=(SETTLE_STEPS,),
-            in_specs=[pl.BlockSpec(back.shape, lambda i, server: (0, 0, 0))],
-            out_specs=pl.BlockSpec((rows, out_cols), lambda i, server: (i, 0)),
-        ),
+        in_specs=[smem, hbm],
+        out_specs=hbm,
+        scratch_shapes=[
+            pltpu.VMEM((units, unit_rows, out_cols), low),
+            pltpu.VMEM((units * unit_rows, out_cols), jnp.float32),
+            dma((units,)),
+            dma((SETTLE_STEPS,)),
+        ],
         name="settle_rows",
     )(unit_server, back)
 

time: 142 us -> 139 us (0.979)
  Pallas kernels: 142 us -> 139 us
    pallas_call x1, Pallas kernels: 139 us -> 136 us  [local(): pl.pallas_call(functools.partial(kernel, n_dp, n_mp, phases), out_shape=j...]
where the time goes in v3:
time: 139 us
  Pallas kernels  139 us (100%)
    pallas_call x1, Pallas kernels, local(): pl.pallas_call(functools.partial(kernel, n_dp, n_mp, phases), out_shape=j...  136 us
    pallas_call x1, Pallas kernels, local(): pl.pallas_call(settle, out_shape=jax.ShapeDtypeStruct((units * unit_rows,...  3.17 us

profile of v3, /device:TPU:1, one launch (start us, length us, event | category | flops | bytes accessed | tf_op | source)
XLA Modules:
  0.0 139.1 jit_solution(12844362878393400797)
XLA Ops:
  0.0 135.9 %attention_backward_exchange.1.back_hbm = bf16[32,32,512]{2,1,0:T(8,128)(2,1)} custom-call(s32[32]{0:T(128)} %server_ref.3, s32[32]{0:T(128)} %place_ref.1, s32[4]{0:T(128)} %length_ref.1, bf16[32,32,512]{2,1,0:T(8,128)(2,1)} %bitcast.4, bf16[32,32,128]{2,1,0:T(8,128)(2,1)} %bitcast.6, bf16[32,32,128]{2,1,0:T(8,128)(2,1)} %bitcast.7, ...), custom_call_target="tpu_custom_call" | custom-call | tf_op jit(solution)/shard_map/attention_backward_exchange/pallas_call | solution.py:459
  135.9 3.2 %settle_rows.1 = f32[1024,512]{1,0:T(8,128)} custom-call(s32[32]{0:T(128)} %server_ref.3, bf16[32,32,512]{2,1,0:T(8,128)(2,1)} %attention_backward_exchange.1.back_hbm), custom_call_target="tpu_custom_call" | custom-call | tf_op jit(solution)/shard_map/settle_rows/pallas_call | solution.py:509

commit v4 on v3

--- a/solution.py
+++ b/solution.py
@@ -17,6 +17,7 @@
 CHUNK_UNITS = 4
 SETTLE_STEPS = 4
 GRID_Y, GRID_X, CORES = 4, 4, 2
+ORDER_STRIDE, ORDER_START = 7, 3
 
 
 def dot(a, b, numbers):
@@ -140,42 +141,49 @@
 
     pl.semaphore_wait(barrier, n_dp - 1 + 2)
 
-    def mixed(i):
-        return 1 + lax.rem(i * 11 + 5, n_dp - 1)
-
-    def table_copy(o):
-        to = peer(o)
-        return pltpu.make_async_remote_copy(
-            src_ref=table_out,
-            dst_ref=table_in.at[me],
-            send_sem=table_send.at[to],
-            recv_sem=table_recv.at[me],
-            device_id={"dp": to},
-            device_id_type=MESH,
-        )
-
-    for p in range(count):
-        for q, copy in loads:
-            if p == q:
-                copy.wait()
-
-        def send_unit(i, carry, p=p):
-            to = peer(mixed(i))
-            stage[p][to] = held[p][inv_smem[0, to]]
-            pltpu.make_async_remote_copy(
-                src_ref=stage[p].at[to],
-                dst_ref=recv[p].at[me],
-                send_sem=a2a_send.at[p, to],
-                recv_sem=a2a_recv.at[p, me],
-                device_id={"dp": to},
-                device_id_type=MESH,
-            ).start()
-            if p == 0:
-                table_copy(mixed(i)).start()
-            return carry
-
-        lax.fori_loop(0, n_dp - 1, send_unit, 0)
-        recv[p][me] = held[p][inv_smem[0, me]]
+    def chip_peer(i, to_core):
+        j = lax.rem(i * ORDER_STRIDE + ORDER_START, GRID_X * GRID_Y)
+        dx = lax.rem(j, GRID_X)
+        dy = j // GRID_X
+        return (
+            lax.rem(y + dy, GRID_Y) * GRID_X + lax.rem(x + dx, GRID_X)
+        ) * CORES + to_core
+
+    for to_core in range(CORES):
+        for p in range(count):
+            if to_core == 0:
+                for q, copy in loads:
+                    if p == q:
+                        copy.wait()
+                recv[p][me] = held[p][inv_smem[0, me]]
+
+            def send_unit(i, carry, p=p, to_core=to_core):
+                to = chip_peer(i, to_core)
+
+                @pl.when(to != me)
+                def _():
+                    stage[p][to] = held[p][inv_smem[0, to]]
+                    pltpu.make_async_remote_copy(
+                        src_ref=stage[p].at[to],
+                        dst_ref=recv[p].at[me],
+                        send_sem=a2a_send.at[p, to],
+                        recv_sem=a2a_recv.at[p, me],
+                        device_id={"dp": to},
+                        device_id_type=MESH,
+                    ).start()
+                    if p == 0:
+                        pltpu.make_async_remote_copy(
+                            src_ref=table_out,
+                            dst_ref=table_in.at[me],
+                            send_sem=table_send.at[to],
+                            recv_sem=table_recv.at[me],
+                            device_id={"dp": to},
+                            device_id_type=MESH,
+                        ).start()
+
+                return carry
+
+            lax.fori_loop(0, GRID_X * GRID_Y, send_unit, 0)
     for copy in weight_loads:
         copy.start()
 
@@ -188,7 +196,7 @@
             recv_sem=table_recv.at[frm],
             device_id={"dp": frm},
             device_id_type=MESH,
-        ).wait()
+        ).wait_recv()
         return carry
 
     lax.fori_loop(1, n_dp, table_arrived, 0)
@@ -257,18 +265,20 @@
             kv_total[doc, 0] = key_grad
             kv_total[doc, 1] = value_grad
 
+    def unit_copy(p, frm):
+        return pltpu.make_async_remote_copy(
+            src_ref=stage[p].at[frm],
+            dst_ref=recv[p].at[frm],
+            send_sem=a2a_send.at[p, frm],
+            recv_sem=a2a_recv.at[p, frm],
+            device_id={"dp": frm},
+            device_id_type=MESH,
+        )
+
     for p in range(count):
 
         def unit_arrived(o, carry, p=p):
-            frm = peer(o)
-            pltpu.make_async_remote_copy(
-                src_ref=stage[p].at[frm],
-                dst_ref=recv[p].at[frm],
-                send_sem=a2a_send.at[p, frm],
-                recv_sem=a2a_recv.at[p, frm],
-                device_id={"dp": frm},
-                device_id_type=MESH,
-            ).wait()
+            unit_copy(p, peer(o)).wait_recv()
             return carry
 
         lax.fori_loop(1, n_dp, unit_arrived, 0)
@@ -376,6 +386,22 @@
 
     lax.fori_loop(0, chunks, last_step, 0)
     own_copy.wait()
+
+    def exchange_done(o, carry):
+        to = peer(o)
+        pltpu.make_async_remote_copy(
+            src_ref=table_out,
+            dst_ref=table_in.at[to],
+            send_sem=table_send.at[to],
+            recv_sem=table_recv.at[to],
+            device_id={"dp": to},
+            device_id_type=MESH,
+        ).wait_send()
+        for p in range(count):
+            unit_copy(p, to).wait_send()
+        return carry
+
+    lax.fori_loop(1, n_dp, exchange_done, 0)
 
     def ring_done(chunk, carry):
         for way in range(2):

time: 139 us -> 130 us (0.935)
  Pallas kernels: 139 us -> 130 us
    pallas_call x1, Pallas kernels: 136 us -> 127 us  [local(): pl.pallas_call(functools.partial(kernel, n_dp, n_mp, phases), out_shape=j...]
where the time goes in v4:
time: 130 us
  Pallas kernels  130 us (100%)
    pallas_call x1, Pallas kernels, local(): pl.pallas_call(functools.partial(kernel, n_dp, n_mp, phases), out_shape=j...  127 us
    pallas_call x1, Pallas kernels, local(): pl.pallas_call(settle, out_shape=jax.ShapeDtypeStruct((units * unit_rows,...  3.17 us

profile of v4, /device:TPU:1, one launch (start us, length us, event | category | flops | bytes accessed | tf_op | source)
XLA Modules:
  0.0 129.9 jit_solution(8978714004318447391)
XLA Ops:
  0.0 126.7 %attention_backward_exchange.1.back_hbm = bf16[32,32,512]{2,1,0:T(8,128)(2,1)} custom-call(s32[32]{0:T(128)} %server_ref.3, s32[32]{0:T(128)} %place_ref.1, s32[4]{0:T(128)} %length_ref.1, bf16[32,32,512]{2,1,0:T(8,128)(2,1)} %bitcast.4, bf16[32,32,128]{2,1,0:T(8,128)(2,1)} %bitcast.6, bf16[32,32,128]{2,1,0:T(8,128)(2,1)} %bitcast.7, ...), custom_call_target="tpu_custom_call" | custom-call | tf_op jit(solution)/shard_map/attention_backward_exchange/pallas_call | solution.py:485
  126.7 3.2 %settle_rows.1 = f32[1024,512]{1,0:T(8,128)} custom-call(s32[32]{0:T(128)} %server_ref.3, bf16[32,32,512]{2,1,0:T(8,128)(2,1)} %attention_backward_exchange.1.back_hbm), custom_call_target="tpu_custom_call" | custom-call | tf_op jit(solution)/shard_map/settle_rows/pallas_call | solution.py:535

commit v5 on v4

--- a/solution.py
+++ b/solution.py
@@ -48,8 +48,8 @@
         table_in,
         inv_vec,
         inv_smem,
-        where_vec,
-        where_smem,
+        place_smem,
+        source_smem,
         weights,
         kv_total,
         grads,
@@ -149,6 +149,20 @@
             lax.rem(y + dy, GRID_Y) * GRID_X + lax.rem(x + dx, GRID_X)
         ) * CORES + to_core
 
+    def send_table(o, carry):
+        to = peer(o)
+        pltpu.make_async_remote_copy(
+            src_ref=table_out,
+            dst_ref=table_in.at[me],
+            send_sem=table_send.at[to],
+            recv_sem=table_recv.at[me],
+            device_id={"dp": to},
+            device_id_type=MESH,
+        ).start()
+        return carry
+
+    lax.fori_loop(1, n_dp, send_table, 0)
+
     for to_core in range(CORES):
         for p in range(count):
             if to_core == 0:
@@ -171,16 +185,6 @@
                         device_id={"dp": to},
                         device_id_type=MESH,
                     ).start()
-                    if p == 0:
-                        pltpu.make_async_remote_copy(
-                            src_ref=table_out,
-                            dst_ref=table_in.at[me],
-                            send_sem=table_send.at[to],
-                            recv_sem=table_recv.at[me],
-                            device_id={"dp": to},
-                            device_id_type=MESH,
-                        ).start()
-
                 return carry
 
             lax.fori_loop(0, GRID_X * GRID_Y, send_unit, 0)
@@ -204,12 +208,9 @@
     wide = lax.broadcasted_iota(jnp.int32, (units, 128), 1)
     tall = lax.broadcasted_iota(jnp.int32, (units, 128), 0)
     place_col = jnp.sum(jnp.where(wide == me, table, 0), axis=1, keepdims=True)
-    source = jnp.max(jnp.where(place_col == wide, tall, 0), axis=0, keepdims=True)
-    where_vec[pl.ds(0, units), :] = jnp.broadcast_to(place_col, (units, 128))
-    where_vec[pl.ds(units, 8), :] = jnp.broadcast_to(source, (8, 128))
-    to_smem = pltpu.make_async_copy(where_vec, where_smem, small_sem.at[1])
-    to_smem.start()
-    to_smem.wait()
+    for n in range(units):
+        place_smem[n] = jnp.max(jnp.where(tall == n, place_col, 0))
+        source_smem[n] = jnp.max(jnp.where(place_col == n, tall, 0))
 
     block = DOC_UNITS * unit_rows
     score_scale = 1.0 / math.sqrt(HEAD)
@@ -217,7 +218,7 @@
 
     def one_doc(p, doc):
         length = length_ref[doc]
-        sources = [where_smem[units, doc * DOC_UNITS + i] for i in range(DOC_UNITS)]
+        sources = [source_smem[doc * DOC_UNITS + i] for i in range(DOC_UNITS)]
 
         def rows(p, at):
             return jnp.concatenate(
@@ -330,7 +331,7 @@
     def first_step(chunk, carry):
         for i in range(CHUNK_UNITS):
             s = peer(n_dp - 1 - (chunk * CHUNK_UNITS + i))
-            lhs[chunk, pl.ds(i * unit_rows, unit_rows), :] = grads[where_smem[s, 0]]
+            lhs[chunk, pl.ds(i * unit_rows, unit_rows), :] = grads[place_smem[s]]
         low = part(chunk, far).astype(jnp.bfloat16)
         for way in range(2):
             ring_send[chunk, way, 0, pl.ds(way * half, half), :] = low[
@@ -468,7 +469,7 @@
     out_cols = out_all // n_mp
     k_cols = q_cols + 2 * kv_cols
     heads = q_cols // HEAD
-    phases = [range(0, heads - 2), range(heads - 2, heads - 1), range(heads - 1, heads)]
+    phases = [range(0, 1), range(1, heads - 1), range(heads - 1, heads)]
     widths = [2 * HEAD * len(p) for p in phases]
     widths[0] += 2 * kv_cols
     chunks = units // CHUNK_UNITS
@@ -495,8 +496,8 @@
             pltpu.VMEM((n_dp, 1, 128), jnp.int32),
             pltpu.VMEM((8, 128), jnp.int32),
             pltpu.SMEM((8, 128), jnp.int32),
-            pltpu.VMEM((units + 8, 128), jnp.int32),
-            pltpu.SMEM((units + 8, 128), jnp.int32),
+            pltpu.SMEM((units,), jnp.int32),
+            pltpu.SMEM((units,), jnp.int32),
             pltpu.VMEM((out_all, k_cols), low),
             pltpu.VMEM((units // DOC_UNITS, 2, DOC_UNITS * unit_rows, HEAD), jnp.float32),
             pltpu.VMEM((units, unit_rows, k_cols), low),

time: 130 us -> 128 us (0.985)
  Pallas kernels: 130 us -> 128 us
    pallas_call x1, Pallas kernels: 127 us -> 125 us  [local(): pl.pallas_call(functools.partial(kernel, n_dp, n_mp, phases), out_shape=j...]
where the time goes in v5:
time: 128 us
  Pallas kernels  128 us (100%)
    pallas_call x1, Pallas kernels, local(): pl.pallas_call(functools.partial(kernel, n_dp, n_mp, phases), out_shape=j...  125 us
    pallas_call x1, Pallas kernels, local(): pl.pallas_call(settle, out_shape=jax.ShapeDtypeStruct((units * unit_rows,...  3.17 us

profile of v5, /device:TPU:1, one launch (start us, length us, event | category | flops | bytes accessed | tf_op | source)
XLA Modules:
  0.0 128.1 jit_solution(2799772357546134527)
XLA Ops:
  0.0 124.9 %attention_backward_exchange.1.back_hbm = bf16[32,32,512]{2,1,0:T(8,128)(2,1)} custom-call(s32[32]{0:T(128)} %server_ref.3, s32[32]{0:T(128)} %place_ref.1, s32[4]{0:T(128)} %length_ref.1, bf16[32,32,512]{2,1,0:T(8,128)(2,1)} %bitcast.4, bf16[32,32,128]{2,1,0:T(8,128)(2,1)} %bitcast.6, bf16[32,32,128]{2,1,0:T(8,128)(2,1)} %bitcast.7, ...), custom_call_target="tpu_custom_call" | custom-call | tf_op jit(solution)/shard_map/attention_backward_exchange/pallas_call | solution.py:486
  124.9 3.2 %settle_rows.1 = f32[1024,512]{1,0:T(8,128)} custom-call(s32[32]{0:T(128)} %server_ref.3, bf16[32,32,512]{2,1,0:T(8,128)(2,1)} %attention_backward_exchange.1.back_hbm), custom_call_target="tpu_custom_call" | custom-call | tf_op jit(solution)/shard_map/settle_rows/pallas_call | solution.py:536

commit v6 on v5

--- a/solution.py
+++ b/solution.py
@@ -15,9 +15,9 @@
 NN = (((1,), (0,)), ((), ()))
 TN = (((0,), (0,)), ((), ()))
 CHUNK_UNITS = 4
-SETTLE_STEPS = 4
+SETTLE_STEPS = 8
 GRID_Y, GRID_X, CORES = 4, 4, 2
-ORDER_STRIDE, ORDER_START = 7, 3
+ORDER_STRIDE, ORDER_START = 11, 3
 
 
 def dot(a, b, numbers):
@@ -427,23 +427,29 @@
     lax.fori_loop(1, n_dp, back_arrived, 0)
 
 
-def settle(server_ref, back_hbm, out_hbm, held, wide, in_sem, out_sem):
+def settle(server_hbm, back_hbm, out_hbm, server, held, wide, server_sem, in_sem, out_sem):
     units, unit_rows = held.shape[:2]
     rows = units * unit_rows // SETTLE_STEPS
-
-    def fetch(u):
-        return pltpu.make_async_copy(back_hbm.at[server_ref[u]], held.at[u], in_sem.at[u])
+    share = units // SETTLE_STEPS
+    table = pltpu.make_async_copy(server_hbm, server, server_sem)
+
+    def fetch(step):
+        part = pl.ds(step * share, share)
+        return pltpu.make_async_copy(back_hbm.at[part], held.at[part], in_sem.at[step])
 
     def emit(step):
         part = pl.ds(step * rows, rows)
         return pltpu.make_async_copy(wide.at[part, :], out_hbm.at[part, :], out_sem.at[step])
 
-    for u in range(units):
-        fetch(u).start()
+    table.start()
     for step in range(SETTLE_STEPS):
-        for u in range(step * units // SETTLE_STEPS, (step + 1) * units // SETTLE_STEPS):
-            fetch(u).wait()
-            wide[pl.ds(u * unit_rows, unit_rows), :] = held[u].astype(jnp.float32)
+        fetch(step).start()
+    table.wait()
+    for step in range(SETTLE_STEPS):
+        fetch(step).wait()
+    for step in range(SETTLE_STEPS):
+        for u in range(step * share, (step + 1) * share):
+            wide[pl.ds(u * unit_rows, unit_rows), :] = held[server[u]].astype(jnp.float32)
         emit(step).start()
     for step in range(SETTLE_STEPS):
         emit(step).wait()
@@ -469,7 +475,7 @@
     out_cols = out_all // n_mp
     k_cols = q_cols + 2 * kv_cols
     heads = q_cols // HEAD
-    phases = [range(0, 1), range(1, heads - 1), range(heads - 1, heads)]
+    phases = [range(h, h + 1) for h in range(heads)]
     widths = [2 * HEAD * len(p) for p in phases]
     widths[0] += 2 * kv_cols
     chunks = units // CHUNK_UNITS
@@ -536,12 +542,14 @@
     return pl.pallas_call(
         settle,
         out_shape=jax.ShapeDtypeStruct((units * unit_rows, out_cols), jnp.float32),
-        in_specs=[smem, hbm],
+        in_specs=[hbm, hbm],
         out_specs=hbm,
         scratch_shapes=[
+            pltpu.SMEM((units,), jnp.int32),
             pltpu.VMEM((units, unit_rows, out_cols), low),
             pltpu.VMEM((units * unit_rows, out_cols), jnp.float32),
-            dma((units,)),
+            dma,
+            dma((SETTLE_STEPS,)),
             dma((SETTLE_STEPS,)),
         ],
         name="settle_rows",

time: 128 us -> 127 us (level)
  no operation moved by 1% of the time
where the time goes in v6:
time: 127 us
  Pallas kernels  127 us (100%)
    pallas_call x1, Pallas kernels, local(): pl.pallas_call(functools.partial(kernel, n_dp, n_mp, phases), out_shape=j...  124 us
    pallas_call x1, Pallas kernels, local(): pl.pallas_call(settle, out_shape=jax.ShapeDtypeStruct((units * unit_rows,...  2.75 us

profile of v6, /device:TPU:1, one launch (start us, length us, event | category | flops | bytes accessed | tf_op | source)
XLA Modules:
  0.0 126.7 jit_solution(9281381348843987001)
XLA Ops:
  0.0 123.9 %attention_backward_exchange.1.back_hbm = bf16[32,32,512]{2,1,0:T(8,128)(2,1)} custom-call(s32[32]{0:T(128)} %server_hbm.1, s32[32]{0:T(128)} %place_ref.1, s32[4]{0:T(128)} %length_ref.1, bf16[32,32,512]{2,1,0:T(8,128)(2,1)} %bitcast.4, bf16[32,32,128]{2,1,0:T(8,128)(2,1)} %bitcast.6, bf16[32,32,128]{2,1,0:T(8,128)(2,1)} %bitcast.7, ...), custom_call_target="tpu_custom_call" | custom-call | tf_op jit(solution)/shard_map/attention_backward_exchange/pallas_call | solution.py:492
  123.9 2.8 %settle_rows.1 = f32[1024,512]{1,0:T(8,128)} custom-call(s32[32]{0:T(128)} %server_hbm.1, bf16[32,32,512]{2,1,0:T(8,128)(2,1)} %attention_backward_exchange.1.back_hbm), custom_call_target="tpu_custom_call" | custom-call | tf_op jit(solution)/shard_map/settle_rows/pallas_call | solution.py:542

commit v7 on v6

--- a/solution.py
+++ b/solution.py
@@ -163,7 +163,33 @@
 
     lax.fori_loop(1, n_dp, send_table, 0)
 
+    def unit_copy(p, frm):
+        return pltpu.make_async_remote_copy(
+            src_ref=stage[p].at[frm],
+            dst_ref=recv[p].at[frm],
+            send_sem=a2a_send.at[p, frm],
+            recv_sem=a2a_recv.at[p, frm],
+            device_id={"dp": frm},
+            device_id_type=MESH,
+        )
+
     for to_core in range(CORES):
+        if to_core > 0:
+
+            @pl.when(core == 1)
+            def _():
+                def gone(i, carry):
+                    to = chip_peer(i, 0)
+
+                    @pl.when(to != me)
+                    def _():
+                        for p in range(count):
+                            unit_copy(p, to).wait_send()
+
+                    return carry
+
+                lax.fori_loop(0, GRID_X * GRID_Y, gone, 0)
+
         for p in range(count):
             if to_core == 0:
                 for q, copy in loads:
@@ -266,16 +292,6 @@
             kv_total[doc, 0] = key_grad
             kv_total[doc, 1] = value_grad
 
-    def unit_copy(p, frm):
-        return pltpu.make_async_remote_copy(
-            src_ref=stage[p].at[frm],
-            dst_ref=recv[p].at[frm],
-            send_sem=a2a_send.at[p, frm],
-            recv_sem=a2a_recv.at[p, frm],
-            device_id={"dp": frm},
-            device_id_type=MESH,
-        )
-
     for p in range(count):
 
         def unit_arrived(o, carry, p=p):
@@ -398,8 +414,12 @@
             device_id={"dp": to},
             device_id_type=MESH,
         ).wait_send()
-        for p in range(count):
-            unit_copy(p, to).wait_send()
+
+        @pl.when((core == 0) | (lax.rem(to, CORES) == 1))
+        def _():
+            for p in range(count):
+                unit_copy(p, to).wait_send()
+
         return carry
 
     lax.fori_loop(1, n_dp, exchange_done, 0)

time: 127 us -> 127 us (level)
  no operation moved by 1% of the time
where the time goes in v7:
time: 127 us
  Pallas kernels  127 us (100%)
    pallas_call x1, Pallas kernels, local(): pl.pallas_call(functools.partial(kernel, n_dp, n_mp, phases), out_shape=j...  124 us
    pallas_call x1, Pallas kernels, local(): pl.pallas_call(settle, out_shape=jax.ShapeDtypeStruct((units * unit_rows,...  2.75 us

profile of v7, /device:TPU:1, one launch (start us, length us, event | category | flops | bytes accessed | tf_op | source)
XLA Modules:
  0.0 126.6 jit_solution(6036646497903119144)
XLA Ops:
  0.0 123.8 %attention_backward_exchange.1.back_hbm = bf16[32,32,512]{2,1,0:T(8,128)(2,1)} custom-call(s32[32]{0:T(128)} %server_hbm.1, s32[32]{0:T(128)} %place_ref.1, s32[4]{0:T(128)} %length_ref.1, bf16[32,32,512]{2,1,0:T(8,128)(2,1)} %bitcast.4, bf16[32,32,128]{2,1,0:T(8,128)(2,1)} %bitcast.6, bf16[32,32,128]{2,1,0:T(8,128)(2,1)} %bitcast.7, ...), custom_call_target="tpu_custom_call" | custom-call | tf_op jit(solution)/shard_map/attention_backward_exchange/pallas_call | solution.py:512
  123.9 2.8 %settle_rows.1 = f32[1024,512]{1,0:T(8,128)} custom-call(s32[32]{0:T(128)} %server_hbm.1, bf16[32,32,512]{2,1,0:T(8,128)(2,1)} %attention_backward_exchange.1.back_hbm), custom_call_target="tpu_custom_call" | custom-call | tf_op jit(solution)/shard_map/settle_rows/pallas_call | solution.py:562
